TPU v7x, 32 devices: a whole 2x2x4 slice. The times are simulated.
32 devices in a mesh: long: 8 (over z, core), grp: 4 (over y, x).
Axes of the slice: x: 2, y: 2, z: 4, core: 2. Of those that a mesh axis runs over, the one named last changes fastest.
Arguments:
- amplitudes: bfloat16 [8192, 12288], P('long', 'grp'), may hold values from -6 to 6
- integrals: bfloat16 [12288, 4096], P('grp', 'long'), may hold values from -0.078125 to 0.078125
- amp_pattern: int32 [128, 192], P('long', 'grp'), may hold values 0 or 1
- int_pattern: int32 [192, 64], P('grp', 'long'), may hold values 0 or 1
- owners: int32 [4], replicated, may hold values from 0 to 7
Outputs:
- ladder: bfloat16 [4, 1024, 4096], P(None, None, ('long', 'grp'))
Inputs may be any that keep to these rules, and one draw needn't show every extreme that they name: `amp_pattern`: tile present (1) or absent (0). `int_pattern`: tile present (1) or absent (0).
All inputs are finite; a program needn't handle non-finite values. No bound on the sum of `amp_pattern` or of `int_pattern` on one device may be relied on, other than what follows from the above.
Results may differ from a plain program's by a relative error of at most 0.001.
Values may be sent and summed in bfloat16 or wider, within the bound.
A program may use at most 192 MiB of HBM per device.

v0:
```python
import jax
import jax.numpy as jnp
from jax import lax
from jax.sharding import PartitionSpec as P

TILE = 64
STEPS = 4


def broadcast(shard, axis, root):
    mine = lax.axis_index(axis) == root
    return lax.psum(jnp.where(mine, shard, jnp.zeros_like(shard)), axis)


def spread_mask(values, pattern):
    row_tiles, col_tiles = pattern.shape
    shaped = values.reshape(row_tiles, TILE, col_tiles, TILE)
    scaled = shaped * pattern.astype(values.dtype)[:, None, :, None]
    return scaled.reshape(row_tiles * TILE, col_tiles * TILE)


def per_device(amplitudes, integrals, amp_pattern, int_pattern, owners):
    sparse_amp = spread_mask(amplitudes, amp_pattern)
    sparse_int = spread_mask(integrals, int_pattern)
    partials = []
    for step in range(STEPS):
        owner_panel = broadcast(sparse_amp, "long", owners[step])
        partial_value = jnp.dot(owner_panel, sparse_int, preferred_element_type=jnp.float32)
        partials.append(
            lax.psum_scatter(partial_value, "grp", scatter_dimension=1, tiled=True).astype(
                jnp.bfloat16
            )
        )
    return jnp.stack(partials, 0)


def solution(mesh):
    placed = (P("long", "grp"), P("grp", "long"), P("long", "grp"), P("grp", "long"), P())
    return jax.shard_map(
        per_device,
        mesh=mesh,
        in_specs=placed,
        out_specs=P(None, None, ("long", "grp")),
        check_vma=False,
    )
```

profile of v0, /device:TPU:0, one launch (start us, length us, event | category | flops | bytes accessed | tf_op | source)
XLA Modules:
  0.0 712.7 jit_solution(11673687661086959189)
XLA Ops:
  6.5 1.5 fusion
  8.0 0.7 convert_element_type.18
  8.7 6.2 mul.22
  14.9 16.3 %mul.23 = bf16[1024,3072]{1,0:T(8,128)(2,1)} reshape(bf16[16,64,48,64]{3,2,1,0:T(8,128)(2,1)} %mul.22) | data formatting | bytes 12582912 | tf_op jit(solution)/shard_map/mul | solution.py:18
  33.9 10.0 %broadcast_select_fusion.3 = (bf16[1024,3072]{1,0:T(8,128)(2,1)}, bf16[1024,3072]{1,0:T(8,128)(2,1)}) fusion(pred[]{:T(512)S(6)} %eq.12, bf16[1024,3072]{1,0:T(8,128)(2,1)} %param.5, bf16[1024,3072]{1,0:T(8,128)(2,1)} %mul.23), kind=kLoop, calls=%fused_computation.3 | loop fusion | flops 6291456 | bytes 25165824 | tf_op jit(solution)/shard_map/jit(_where)/select_n | solution.py:12
  43.9 8.3 %broadcast_select_fusion.2 = (bf16[1024,3072]{1,0:T(8,128)(2,1)}, bf16[1024,3072]{1,0:T(8,128)(2,1)}, bf16[1024,3072]{1,0:T(8,128)(2,1)}) fusion(bf16[1024,3072]{1,0:T(8,128)(2,1)} %get-tuple-element.10, pred[]{:T(512)S(6)} %eq.13, pred[]{:T(512)S(6)} %eq.14, pred[]{:T(512)S(6)} %eq.15), kind=kLoop, calls=%fused_computation.2 | loop fusion | flops 9437184 | bytes 25165828 | tf_op jit(solution)/shard_map/jit(_where)/select_n | solution.py:12
  52.2 0.0 reduce-scatter.11.cloned.1.call-start
  52.3 0.6 copy-done.1
  52.9 0.1 copy.6
  53.0 3.5 mul.25
  56.4 8.3 %mul.26 = bf16[3072,512]{1,0:T(8,128)(2,1)S(1)} reshape(bf16[48,64,8,64]{3,2,1,0:T(8,128)(2,1)} %mul.25) | data formatting | bytes 6291456 | tf_op jit(solution)/shard_map/mul | solution.py:18
  64.7 4.4 mul.27
  69.1 476.5 %all-reduce.3.cloned.1.call-done = (bf16[1024,3072]{1,0:T(8,128)(2,1)}, bf16[1024,3072]{1,0:T(8,128)(2,1)}, bf16[1024,3072]{1,0:T(8,128)(2,1)}, bf16[1024,3072]{1,0:T(8,128)(2,1)}) async-done(((bf16[1024,3072]{1,0:T(8,128)(2,1)}, bf16[1024,3072]{1,0:T(8,128)(2,1)}, bf16[1024,3072]{1,0:T(8,128)(2,1)}, bf16[1024,3072]{1,0:T(8,128)(2,1)}), (bf16[1024,3072]{1,0:T(8,128)(2,1)}, bf16[1024,3072]{1,0:T(8,128)(2,1)}, ...) | async-done | bytes 25165840 | tf_op jit(solution)/shard_map/psum | solution.py:12
  545.6 8.6 %fusion.4 = f32[1024,512]{1,0:T(8,128)} fusion(bf16[1024,3072]{1,0:T(8,128)(2,1)} %get-tuple-element.5, bf16[3072,512]{1,0:T(8,128)(2,1)} %mul.27), kind=kOutput, calls=%fused_computation.13 | convolution fusion | flops 3221225472 | bytes 11534336 | tf_op jit(solution)/shard_map/dot_general | solution.py:28
  554.2 0.0 reduce-scatter.11.cloned.1.call-update
  554.3 0.0 reduce-scatter.9.cloned.1.call-start
  554.3 7.5 %fusion.3 = f32[1024,512]{1,0:T(8,128)} fusion(bf16[1024,3072]{1,0:T(8,128)(2,1)} %get-tuple-element.6, bf16[3072,512]{1,0:T(8,128)(2,1)S(1)} %copy-done), kind=kOutput, calls=%fused_computation.12 | convolution fusion | flops 3221225472 | bytes 11534336 | tf_op jit(solution)/shard_map/dot_general | solution.py:28
  561.8 0.0 reduce-scatter.9.cloned.1.call-update
  561.8 0.2 reduce-scatter.7.cloned.1.call-start
  562.1 7.5 %fusion.2 = f32[1024,512]{1,0:T(8,128)} fusion(bf16[1024,3072]{1,0:T(8,128)(2,1)} %get-tuple-element.7, bf16[3072,512]{1,0:T(8,128)(2,1)S(1)} %copy-done), kind=kOutput, calls=%fused_computation.11 | convolution fusion | flops 3221225472 | bytes 11534336 | tf_op jit(solution)/shard_map/dot_general | solution.py:28
  569.6 0.0 reduce-scatter.7.cloned.1.call-update
  569.6 0.0 reduce-scatter.5.cloned.1.call-start
  569.7 7.7 %fusion.1 = f32[1024,512]{1,0:T(8,128)} fusion(bf16[1024,3072]{1,0:T(8,128)(2,1)} %get-tuple-element.8, bf16[3072,512]{1,0:T(8,128)(2,1)S(1)} %copy-done), kind=kOutput, calls=%fused_computation.10 | convolution fusion | flops 3221225472 | bytes 11534336 | tf_op jit(solution)/shard_map/dot_general | solution.py:28
  577.4 12.3 %reduce-scatter.11.cloned.1.call-done = f32[1024,128]{1,0:T(8,128)} async-done(((f32[1024,512]{1,0:T(8,128)}), f32[1024,128]{1,0:T(8,128)}) %reduce-scatter.11.cloned.1.call-update) | async-done | bytes 524304 | tf_op jit(solution)/shard_map/reduce_scatter | solution.py:30
  589.8 1.1 convert_bitcast_fusion
  590.8 37.1 %reduce-scatter.9.cloned.1.call-done = f32[1024,128]{1,0:T(8,128)} async-done(((f32[1024,512]{1,0:T(8,128)}), f32[1024,128]{1,0:T(8,128)}) %reduce-scatter.9.cloned.1.call-update) | async-done | bytes 524304 | tf_op jit(solution)/shard_map/reduce_scatter | solution.py:30
  627.9 1.1 convert_bitcast_fusion.1
  629.0 37.0 %reduce-scatter.7.cloned.1.call-done = f32[1024,128]{1,0:T(8,128)} async-done(((f32[1024,512]{1,0:T(8,128)}), f32[1024,128]{1,0:T(8,128)}) %reduce-scatter.7.cloned.1.call-update) | async-done | bytes 524304 | tf_op jit(solution)/shard_map/reduce_scatter | solution.py:30
  666.0 1.1 convert_bitcast_fusion.2
  667.0 37.0 %reduce-scatter.5.cloned.1.call-done = f32[1024,128]{1,0:T(8,128)} async-done(((f32[1024,512]{1,0:T(8,128)}), f32[1024,128]{1,0:T(8,128)}) %reduce-scatter.5.cloned.1.call-update) | async-done | bytes 524304 | tf_op jit(solution)/shard_map/reduce_scatter | solution.py:30
  704.0 1.1 convert_bitcast_fusion.3
  705.1 1.1 pad_maximum_fusion
  (7 shorter events, 0.0 us)
Async XLA Ops:
  6.5 539.1 %all-reduce.3.cloned.1.call-start = ((), (), s32[]{:S(2)}) async-start(), calls=%async_computation.8 | async-start | bytes 50331648 | tf_op jit(solution)/shard_map/psum | solution.py:12
  52.2 0.7 copy-start.1
  52.2 537.5 %reduce-scatter.11.cloned.1.call-start = ((), (), s32[]{:S(2)}) async-start(), calls=%async_computation.7 | async-start | bytes 2621440 | tf_op jit(solution)/shard_map/reduce_scatter | solution.py:30
  545.6 8.7 %copy-start = (bf16[3072,512]{1,0:T(8,128)(2,1)S(1)}, bf16[3072,512]{1,0:T(8,128)(2,1)}, u32[]{:S(2)}) copy-start(bf16[3072,512]{1,0:T(8,128)(2,1)} %mul.27) | copy-start | bytes 9437188
  554.3 73.7 %reduce-scatter.9.cloned.1.call-start = ((), (), s32[]{:S(2)}) async-start(), calls=%async_computation.6 | async-start | bytes 2621440 | tf_op jit(solution)/shard_map/reduce_scatter | solution.py:30
  561.8 104.2 %reduce-scatter.7.cloned.1.call-start = ((), (), s32[]{:S(2)}) async-start(), calls=%async_computation.5 | async-start | bytes 2621440 | tf_op jit(solution)/shard_map/reduce_scatter | solution.py:30
  569.6 134.4 %reduce-scatter.5.cloned.1.call-start = ((), (), s32[]{:S(2)}) async-start(), calls=%async_computation.4 | async-start | bytes 2621440 | tf_op jit(solution)/shard_map/reduce_scatter | solution.py:30
Sparse Core Ops, SparseCore 0:
  52.3 493.2 all-reduce.2
  554.4 35.3 reduce-scatter.10
  592.7 35.1 reduce-scatter.8
  630.8 35.1 reduce-scatter.6
  668.8 35.1 reduce-scatter.4
where the time goes:
time: 714 us; the launch traced here: 713 us
  waiting for transfers between devices  600 us (84%)
  local copies, waits for them, and re-layouts  36.4 us (5%)
  matrix products  31.4 us (4%)
  other arithmetic  28.8 us (4%)
  between operations  15.8 us (2%)
    psum x1, waiting for transfers between devices, broadcast(): return lax.psum(jnp.where(mine, shard, jnp.zeros_like(shard)), axis)  476 us
    reduce_scatter x4, waiting for transfers between devices, per_device(): lax.psum_scatter(partial_value, 'grp', scatter_dimension=1, tiled=True)  123 us
    mul x4, local copies, waits for them, and re-layouts, spread_mask(): scaled = shaped * pattern.astype(values.dtype)[:, None, :, None]  34.3 us
    dot_general x4, matrix products, per_device(): jnp.dot(owner_panel, sparse_int, preferred_element_type=jnp.float32)  31.4 us
    select_n x2, other arithmetic, broadcast(): return lax.psum(jnp.where(mine, shard, jnp.zeros_like(shard)), axis)  18.3 us
  transfers between devices with their start and end apart: 5, of which 5 were waited for; matrix products, arithmetic and copies ran while one was open for 6% of the time, Pallas kernels for 0%

commit v1 on v0

v1 whole, which is shorter than its diff:
```python
import functools

import jax
import jax.numpy as jnp
from jax import lax
from jax.experimental import pallas as pl
from jax.experimental.pallas import tpu as pltpu
from jax.sharding import PartitionSpec as P

TILE = 64
LANES = 128
CHUNKS = 4
SHARE = (3, 5)
BLOCK = 256


def broadcast(shard, axis, root):
    mine = lax.axis_index(axis) == root
    return lax.psum(jnp.where(mine, shard, jnp.zeros_like(shard)), axis)


def spread(pattern, dtype):
    row_tiles, col_tiles = pattern.shape
    down = jnp.arange(row_tiles * TILE)[:, None] // TILE == jnp.arange(row_tiles)[None, :]
    across = jnp.arange(col_tiles * TILE)[None, :] // TILE == jnp.arange(col_tiles)[:, None]
    rows = jnp.dot(down.astype(dtype), pattern.astype(dtype), preferred_element_type=dtype)
    return jnp.dot(rows, across.astype(dtype), preferred_element_type=dtype)


def dense_path(amplitudes, sparse_int, amp_pattern, owners):
    sparse_amp = amplitudes * spread(amp_pattern, amplitudes.dtype)

    def step(_, owner):
        panel = broadcast(sparse_amp, "long", owner)
        partial_value = jnp.dot(panel, sparse_int, preferred_element_type=jnp.float32)
        total = lax.psum_scatter(partial_value, "grp", scatter_dimension=1, tiled=True)
        return None, total.astype(amplitudes.dtype)

    return lax.scan(step, None, owners)[1]


def halves(dtype):
    lane = lax.broadcasted_iota(jnp.int32, (TILE, LANES), 1)
    left = (lane < TILE).astype(jnp.float32).astype(dtype)
    right = (lane >= TILE).astype(jnp.float32).astype(dtype)
    return left, right


def pack_kernel(where_ref, a_ref, out_ref):
    left, right = halves(out_ref.dtype)

    def tile(slot, parity):
        row = pl.multiple_of(where_ref[2 * parity, slot], TILE)
        col = pl.multiple_of(where_ref[2 * parity + 1, slot], LANES)
        return a_ref[pl.ds(row, TILE), pl.ds(col, LANES)]

    def body(slot, _):
        to = pl.multiple_of(slot * TILE, TILE)
        out_ref[pl.ds(to, TILE), :] = tile(slot, 0) * left + tile(slot, 1) * right
        return 0

    lax.fori_loop(0, out_ref.shape[0] // TILE, body, 0, unroll=4)


def pack(amplitudes, spots, slots):
    return pl.pallas_call(
        pack_kernel,
        out_shape=jax.ShapeDtypeStruct((slots * TILE, LANES), amplitudes.dtype),
        grid_spec=pltpu.PrefetchScalarGridSpec(
            num_scalar_prefetch=1,
            grid=(1,),
            in_specs=[pl.BlockSpec(amplitudes.shape, lambda i, w: (0, 0))],
            out_specs=pl.BlockSpec((slots * TILE, LANES), lambda i, w: (0, 0)),
        ),
    )(spots, amplitudes)


def multiply_kernel(pairs, rank_ref, packed_ref, b_ref, out_ref, dense_ref):
    left, right = halves(dense_ref.dtype)
    row_tiles = dense_ref.shape[0] // TILE
    first = pl.program_id(0) * row_tiles * pairs

    def body(row, _):
        to = pl.multiple_of(row * TILE, TILE)
        for col in range(pairs):
            at = first + row * pairs + col
            even = pl.multiple_of(rank_ref[0, at], TILE)
            odd = pl.multiple_of(rank_ref[1, at], TILE)
            dense_ref[pl.ds(to, TILE), col * LANES : (col + 1) * LANES] = (
                packed_ref[pl.ds(even, TILE), :] * left + packed_ref[pl.ds(odd, TILE), :] * right
            )
        return 0

    lax.fori_loop(0, row_tiles, body, 0)
    out_ref[...] = jnp.dot(dense_ref[...], b_ref[...], preferred_element_type=jnp.float32)


def multiply(packed, ranks, b, rows):
    depth, cols = b.shape
    block = min(BLOCK, rows)
    return pl.pallas_call(
        functools.partial(multiply_kernel, depth // LANES),
        out_shape=jax.ShapeDtypeStruct((rows, cols), jnp.float32),
        grid_spec=pltpu.PrefetchScalarGridSpec(
            num_scalar_prefetch=1,
            grid=(rows // block,),
            in_specs=[
                pl.BlockSpec(packed.shape, lambda i, r: (0, 0)),
                pl.BlockSpec(b.shape, lambda i, r: (0, 0)),
            ],
            out_specs=pl.BlockSpec((block, cols), lambda i, r: (i, 0)),
            scratch_shapes=[pltpu.VMEM((block, depth), packed.dtype)],
        ),
        cost_estimate=pl.CostEstimate(
            flops=2 * rows * depth * cols,
            bytes_accessed=packed.size * 2 + b.size * 2 + rows * cols * 4,
            transcendentals=0,
        ),
    )(ranks, packed, b)


def by_parity(pattern):
    *lead, row_tiles, col_tiles = pattern.shape
    flat = pattern.reshape(*lead, row_tiles * col_tiles // 2, 2)
    flat = jnp.swapaxes(flat, -1, -2)
    return flat, jnp.cumsum(flat, axis=-1)


def per_device(long, grp, amplitudes, integrals, amp_pattern, int_pattern, owners):
    steps = owners.shape[0]
    chips = long // 2
    rows, depth = amplitudes.shape
    pairs = depth // LANES
    slots = -(-(rows // TILE) * pairs * SHARE[0] // (SHARE[1] * 2 * CHUNKS)) * 2 * CHUNKS
    half = slots // 2 * TILE
    piece = half // CHUNKS

    me = lax.axis_index("long")
    chip, core = me // 2, me % 2
    swap = [(i, i ^ 1) for i in range(long)]
    up = [(i, i + 2) for i in range(long - 2)]
    down = [(i + 2, i) for i in range(long - 2)]

    _, count = by_parity(amp_pattern)
    spot = jnp.sum(count[:, None, :] <= jnp.arange(slots)[None, :, None], axis=-1)
    spot = jnp.minimum(spot, count.shape[-1] - 1)
    spots = jnp.stack([spot // pairs * TILE, spot % pairs * LANES], 1).reshape(4, slots)
    packed = pack(amplitudes, spots.astype(jnp.int32), slots)

    patterns = lax.all_gather(amp_pattern, ("long", "grp"))
    patterns = patterns.reshape(long, grp, *amp_pattern.shape)[owners]
    full = jnp.any(jnp.sum(by_parity(patterns)[0], axis=-1) > slots)
    here, count = by_parity(lax.dynamic_index_in_dim(patterns, lax.axis_index("grp"), 1, False))
    rank = (count - 1 + core * (slots // 2)) % slots
    ranks = jnp.where(here > 0, jnp.minimum(rank, slots), slots).astype(jnp.int32) * TILE

    sparse_int = integrals * spread(int_pattern, integrals.dtype)

    keep = lax.dynamic_slice_in_dim(packed, core * half, half, 0)
    give = lax.dynamic_slice_in_dim(packed, (1 - core) * half, half, 0)
    gain = lax.ppermute(give, "long", swap)

    def own(number):
        at = number % CHUNKS * piece
        mine = owners[number // CHUNKS] % 2 == core
        return jnp.where(
            mine,
            lax.dynamic_slice_in_dim(keep, at, piece, 0),
            lax.dynamic_slice_in_dim(gain, at, piece, 0),
        )

    pieces = steps * CHUNKS

    def outgoing(number, carried):
        number = jnp.clip(number, 0, pieces - 1)
        mine = owners[number // CHUNKS] // 2 == chip
        return own(number) if carried is None else jnp.where(mine, own(number), carried)

    rose, fell = [], []
    for turn in range(pieces + chips - 2):
        rising = outgoing(turn - chip, rose[-1] if rose else None)
        falling = outgoing(turn - (chips - 1 - chip), fell[-1] if fell else None)
        rose.append(lax.ppermute(rising, "long", up))
        fell.append(lax.ppermute(falling, "long", down))

    results = []
    for step in range(steps):
        source = owners[step] // 2
        kept = []
        for number in range(step * CHUNKS, (step + 1) * CHUNKS):
            value = own(number)
            for place in range(chips):
                if place > 0:
                    below = (chip == place) & (source < chip)
                    value = jnp.where(below, rose[number + place - 1], value)
                if place < chips - 1:
                    above = (chip == place) & (source > chip)
                    value = jnp.where(above, fell[number + chips - 2 - place], value)
            kept.append(value)
        other = [lax.ppermute(value, "long", swap) for value in kept]
        nothing = jnp.zeros((TILE, LANES), amplitudes.dtype)
        panel = jnp.concatenate(kept + other + [nothing], 0)
        partial_value = multiply(panel, ranks[step], sparse_int, rows)
        total = lax.psum_scatter(partial_value, "grp", scatter_dimension=1, tiled=True)
        results.append(total.astype(amplitudes.dtype))
    quick = jnp.stack(results, 0)

    return lax.cond(
        full,
        lambda: dense_path(amplitudes, sparse_int, amp_pattern, owners),
        lambda: quick,
    )


def solution(mesh):
    placed = (P("long", "grp"), P("grp", "long"), P("long", "grp"), P("grp", "long"), P())
    return jax.shard_map(
        functools.partial(per_device, mesh.shape["long"], mesh.shape["grp"]),
        mesh=mesh,
        in_specs=placed,
        out_specs=P(None, None, ("long", "grp")),
        check_vma=False,
    )
```

time: 714 us -> 597 us (0.84); the launches traced: 713 us -> 586 us
  waiting for transfers between devices: 600 us -> 164 us
  between operations: 15.8 us -> 118 us
  starting transfers between devices: 0.35 us -> 82.5 us
  blocking collectives: 0 us -> 76 us
  Pallas kernels: 0 us -> 53.3 us
  other arithmetic: 28.8 us -> 60 us
  matrix products: 31.4 us -> 5.1 us
  local copies, waits for them, and re-layouts: 36.4 us -> 26.7 us
    psum x1 -> x0, waiting for transfers between devices: 476 us -> none  [broadcast(): return lax.psum(jnp.where(mine, shard, jnp.zeros_like(shard)), axis)]
    ppermute x0 -> x53, waiting for transfers between devices: none -> 130 us  [the longest x18 79 us: per_device(): rose.append(lax.ppermute(rising, 'long', up))]
    reduce_scatter x4, waiting for transfers between devices: 123 us -> 33.8 us  [per_device(): lax.psum_scatter(partial_value, 'grp', scatter_dimension=1, tiled=True)]
    ppermute x0 -> x53, starting transfers between devices: none -> 82.3 us  [the longest x18 57.4 us: per_device(): rose.append(lax.ppermute(rising, 'long', up))]
    all_gather x0 -> x1, blocking collectives: none -> 76 us  [per_device(): patterns = lax.all_gather(amp_pattern, ('long', 'grp'))]
    pallas_call x0 -> x5, Pallas kernels: none -> 53.3 us  [the longest x4 45 us: multiply(): pl.pallas_call(functools.partial(multiply_kernel, depth // LANES), out_sh...]
    mul x4 -> x0, local copies, waits for them, and re-layouts: 34.3 us -> none  [spread_mask(): scaled = shaped * pattern.astype(values.dtype)[:, None, :, None]]
    dot_general x4 -> x1, matrix products: 31.4 us -> 5.1 us  [spread(): return jnp.dot(rows, across.astype(dtype), preferred_element_type=dtype)]
  transfers between devices with their start and end apart: 5 -> 57, of which waited for: 5 -> 28; matrix products, arithmetic and copies ran while one was open for 6% -> 13% of each run, Pallas kernels for 0% -> 8%
where the time goes in v1:
time: 597 us; the launch traced here: 586 us
  waiting for transfers between devices  164 us (27%)
  between operations  118 us (20%)
  starting transfers between devices  82.5 us (14%)
  blocking collectives  76 us (13%)
  other arithmetic  60 us (10%)
  Pallas kernels  53.3 us (9%)
  local copies, waits for them, and re-layouts  26.7 us (4%)
    ppermute x18, waiting for transfers between devices, per_device(): rose.append(lax.ppermute(rising, 'long', up))  79 us
    all_gather x1, blocking collectives, per_device(): patterns = lax.all_gather(amp_pattern, ('long', 'grp'))  76 us
    ppermute x18, starting transfers between devices, per_device(): rose.append(lax.ppermute(rising, 'long', up))  57.4 us
    ppermute x18, waiting for transfers between devices, per_device(): fell.append(lax.ppermute(falling, 'long', down))  50.2 us
    pallas_call x4, Pallas kernels, multiply(): pl.pallas_call(functools.partial(multiply_kernel, depth // LANES), out_sh...  45 us
    reduce_scatter x4, waiting for transfers between devices, per_device(): lax.psum_scatter(partial_value, 'grp', scatter_dimension=1, tiled=True)  33.8 us
    unnamed x17, other arithmetic  24.5 us
    select_n x19, other arithmetic, outgoing(): jnp.where(mine, own(number), carried)  24.2 us
  transfers between devices with their start and end apart: 57, of which 28 were waited for; matrix products, arithmetic and copies ran while one was open for 13% of the time, Pallas kernels for 8%

profile of v1, /device:TPU:0, one launch (start us, length us, event | category | flops | bytes accessed | tf_op | source)
XLA Modules:
  0.0 585.6 jit_solution(3857001381438165005)
XLA Ops:
  9.4 8.3 %shard_map.57 = bf16[14848,128]{1,0:T(8,128)(2,1)} custom-call(s32[4,232]{1,0:T(4,128)} %reshape.270.where_ref, bf16[1024,3072]{1,0:T(8,128)(2,1)} %a_ref.1), custom_call_target="tpu_custom_call" | custom-call | tf_op jit(solution)/shard_map/pallas_call | solution.py:66
  126.2 76.0 %all-gather = s32[512,48]{1,0:T(8,128)S(1)} all-gather(s32[16,48]{1,0:T(8,128)S(1)} %copy-done.32), channel_id=2, replica_groups=mesh['long'=8,'grp'=4] {'long','grp'}, dimensions={0}, use_global_device_ids=true | all-gather | bytes 101376 | tf_op jit(solution)/shard_map/all_gather | solution.py:150
  209.9 5.9 %collective-permute-done.1 = bf16[1856,128]{1,0:T(8,128)(2,1)S(1)} collective-permute-done((bf16[1856,128]{1,0:T(8,128)(2,1)S(1)}, bf16[1856,128]{1,0:T(8,128)(2,1)S(1)}, u32[]{:S(2)}, u32[]{:S(2)}) %collective-permute-start.1) | collective-permute-done | bytes 475168 | tf_op jit(solution)/shard_map/ppermute | solution.py:183
  218.0 4.4 collective-permute-start.2
  233.2 4.6 collective-permute-start.3
  237.8 5.1 convolution_multiply_fusion.1.b_ref
  246.9 4.3 collective-permute-start.7
  257.3 5.0 collective-permute-done.8
  264.1 4.6 collective-permute-start.9
  277.1 4.4 collective-permute-start.11
  287.7 4.4 collective-permute-done.12
  302.6 11.3 %shard_map.58 = f32[1024,512]{1,0:T(8,128)} custom-call(s32[2,384]{1,0:T(2,128)} %get-tuple-element.123.rank_ref, bf16[14912,128]{1,0:T(8,128)(2,1)} %constant_dynamic-update-slice_fusion.packed_ref, bf16[3072,512]{1,0:T(8,128)(2,1)} %convolution_multiply_fusion.1.b_ref), custom_call_target="tpu_custom_call" | custom-call | flops 3221225472 | bytes 9060352 | tf_op jit(solution)/shard_map/pallas_call | solution.py:101
  315.8 4.9 collective-permute-start.19
  323.5 7.4 %collective-permute-done.19 = bf16[1856,128]{1,0:T(8,128)(2,1)S(1)} collective-permute-done((bf16[1856,128]{1,0:T(8,128)(2,1)S(1)}, bf16[1856,128]{1,0:T(8,128)(2,1)S(1)}, u32[]{:S(2)}, u32[]{:S(2)}) %collective-permute-start.19) | collective-permute-done | bytes 475168 | tf_op jit(solution)/shard_map/ppermute | solution.py:183
  330.9 4.3 collective-permute-done.20
  340.5 6.8 %collective-permute-done.21 = bf16[1856,128]{1,0:T(8,128)(2,1)S(1)} collective-permute-done((bf16[1856,128]{1,0:T(8,128)(2,1)S(1)}, bf16[1856,128]{1,0:T(8,128)(2,1)S(1)}, u32[]{:S(2)}, u32[]{:S(2)}) %collective-permute-start.21) | collective-permute-done | bytes 475168 | tf_op jit(solution)/shard_map/ppermute | solution.py:183
  356.8 6.1 %collective-permute-done.23 = bf16[1856,128]{1,0:T(8,128)(2,1)S(1)} collective-permute-done((bf16[1856,128]{1,0:T(8,128)(2,1)S(1)}, bf16[1856,128]{1,0:T(8,128)(2,1)S(1)}, u32[]{:S(2)}, u32[]{:S(2)}) %collective-permute-start.23) | collective-permute-done | bytes 475168 | tf_op jit(solution)/shard_map/ppermute | solution.py:183
  374.9 6.9 %collective-permute-done.29 = bf16[1856,128]{1,0:T(8,128)(2,1)S(1)} collective-permute-done((bf16[1856,128]{1,0:T(8,128)(2,1)S(1)}, bf16[1856,128]{1,0:T(8,128)(2,1)S(1)}, u32[]{:S(2)}, u32[]{:S(2)}) %collective-permute-start.29) | collective-permute-done | bytes 475168 | tf_op jit(solution)/shard_map/ppermute | solution.py:183
  381.8 4.2 collective-permute-done.30
  393.9 11.2 %shard_map.59 = f32[1024,512]{1,0:T(8,128)} custom-call(s32[2,384]{1,0:T(2,128)} %get-tuple-element.126.rank_ref, bf16[14912,128]{1,0:T(8,128)(2,1)} %constant_dynamic-update-slice_fusion.9.packed_ref, bf16[3072,512]{1,0:T(8,128)(2,1)} %convolution_multiply_fusion.1.b_ref), custom_call_target="tpu_custom_call" | custom-call | flops 3221225472 | bytes 9060352 | tf_op jit(solution)/shard_map/pallas_call | solution.py:101
  407.3 4.6 collective-permute-start.33
  416.2 6.5 %collective-permute-done.33 = bf16[1856,128]{1,0:T(8,128)(2,1)S(1)} collective-permute-done((bf16[1856,128]{1,0:T(8,128)(2,1)S(1)}, bf16[1856,128]{1,0:T(8,128)(2,1)S(1)}, u32[]{:S(2)}, u32[]{:S(2)}) %collective-permute-start.33) | collective-permute-done | bytes 475168 | tf_op jit(solution)/shard_map/ppermute | solution.py:183
  422.7 4.2 collective-permute-done.34
  432.2 7.3 %collective-permute-done.35 = bf16[1856,128]{1,0:T(8,128)(2,1)S(1)} collective-permute-done((bf16[1856,128]{1,0:T(8,128)(2,1)S(1)}, bf16[1856,128]{1,0:T(8,128)(2,1)S(1)}, u32[]{:S(2)}, u32[]{:S(2)}) %collective-permute-start.35) | collective-permute-done | bytes 475168 | tf_op jit(solution)/shard_map/ppermute | solution.py:183
  452.4 6.0 %collective-permute-done.41 = bf16[1856,128]{1,0:T(8,128)(2,1)S(1)} collective-permute-done((bf16[1856,128]{1,0:T(8,128)(2,1)S(1)}, bf16[1856,128]{1,0:T(8,128)(2,1)S(1)}, u32[]{:S(2)}, u32[]{:S(2)}) %collective-permute-start.41) | collective-permute-done | bytes 475168 | tf_op jit(solution)/shard_map/ppermute | solution.py:183
  458.4 4.2 collective-permute-done.42
  469.7 11.2 %shard_map.60 = f32[1024,512]{1,0:T(8,128)} custom-call(s32[2,384]{1,0:T(2,128)} %get-tuple-element.125.rank_ref, bf16[14912,128]{1,0:T(8,128)(2,1)} %constant_dynamic-update-slice_fusion.18.packed_ref, bf16[3072,512]{1,0:T(8,128)(2,1)} %convolution_multiply_fusion.1.b_ref), custom_call_target="tpu_custom_call" | custom-call | flops 3221225472 | bytes 9060352 | tf_op jit(solution)/shard_map/pallas_call | solution.py:101
  492.6 6.9 %collective-permute-done.45 = bf16[1856,128]{1,0:T(8,128)(2,1)S(1)} collective-permute-done((bf16[1856,128]{1,0:T(8,128)(2,1)S(1)}, bf16[1856,128]{1,0:T(8,128)(2,1)S(1)}, u32[]{:S(2)}, u32[]{:S(2)}) %collective-permute-start.45) | collective-permute-done | bytes 475168 | tf_op jit(solution)/shard_map/ppermute | solution.py:183
  509.0 7.1 %collective-permute-done.47 = bf16[1856,128]{1,0:T(8,128)(2,1)S(1)} collective-permute-done((bf16[1856,128]{1,0:T(8,128)(2,1)S(1)}, bf16[1856,128]{1,0:T(8,128)(2,1)S(1)}, u32[]{:S(2)}, u32[]{:S(2)}) %collective-permute-start.47) | collective-permute-done | bytes 475168 | tf_op jit(solution)/shard_map/ppermute | solution.py:183
  516.1 4.1 collective-permute-done.48
  525.4 11.2 %shard_map.61 = f32[1024,512]{1,0:T(8,128)} custom-call(s32[2,384]{1,0:T(2,128)} %get-tuple-element.124.rank_ref, bf16[14912,128]{1,0:T(8,128)(2,1)} %constant_dynamic-update-slice_fusion.27.packed_ref, bf16[3072,512]{1,0:T(8,128)(2,1)} %convolution_multiply_fusion.1.b_ref), custom_call_target="tpu_custom_call" | custom-call | flops 3221225472 | bytes 9060352 | tf_op jit(solution)/shard_map/pallas_call | solution.py:101
  542.5 33.7 %reduce-scatter.12.cloned.1.call-done = f32[1024,128]{1,0:T(8,128)} async-done(((f32[1024,512]{1,0:T(8,128)}), f32[1024,128]{1,0:T(8,128)}) %reduce-scatter.12.cloned.1.call-update) | async-done | bytes 524304 | tf_op jit(solution)/shard_map/reduce_scatter | solution.py:204
  (261 shorter events, 170.8 us)
Async XLA Ops:
  6.5 532.7 %reduce-scatter.6.cloned.1.call-start = ((), (), s32[]{:S(2)}) async-start(), calls=%async_computation.5 | async-start | bytes 2621440 | tf_op jit(solution)/shard_map/reduce_scatter | solution.py:204
  26.1 96.7 %collective-permute-start.4 = (bf16[1856,128]{1,0:T(8,128)(2,1)S(1)}, bf16[1856,128]{1,0:T(8,128)(2,1)S(1)}, u32[]{:S(2)}, u32[]{:S(2)}) collective-permute-start(bf16[1856,128]{1,0:T(8,128)(2,1)S(1)} %dynamic-slice_select_fusion), channel_id=1, source_target_pairs={{8,0},{12,4},{16,8},{20,12},{24,16},{28,20},{9,1},{13,5},{17,9},{2... | collective-permute-start | bytes 1425416 | tf_op jit(solution)/shard_map/ppermute | solution.py:184
  124.8 80.9 %collective-permute-start.5 = (bf16[1856,128]{1,0:T(8,128)(2,1)S(1)}, bf16[1856,128]{1,0:T(8,128)(2,1)S(1)}, u32[]{:S(2)}, u32[]{:S(2)}) collective-permute-start(bf16[1856,128]{1,0:T(8,128)(2,1)S(1)} %select_select_fusion.47), channel_id=1, source_target_pairs={{8,0},{12,4},{16,8},{20,12},{24,16},{28,20},{9,1},{13,5},{17,9},{2... | collective-permute-start | bytes 1425416 | tf_op jit(solution)/shard_map/ppermute | solution.py:184
  253.9 43.5 %collective-permute-start.13 = (bf16[1856,128]{1,0:T(8,128)(2,1)S(1)}, bf16[1856,128]{1,0:T(8,128)(2,1)S(1)}, u32[]{:S(2)}, u32[]{:S(2)}) collective-permute-start(bf16[1856,128]{1,0:T(8,128)(2,1)S(1)} %get-tuple-element.66), channel_id=1, source_target_pairs={{0,4},{4,0},{8,12},{12,8},{16,20},{20,16},{24,28},{28,24},{1,5},{5... | collective-permute-start | bytes 1425416 | tf_op jit(solution)/shard_map/ppermute | solution.py:200
  270.0 29.6 %collective-permute-start.14 = (bf16[1856,128]{1,0:T(8,128)(2,1)S(1)}, bf16[1856,128]{1,0:T(8,128)(2,1)S(1)}, u32[]{:S(2)}, u32[]{:S(2)}) collective-permute-start(bf16[1856,128]{1,0:T(8,128)(2,1)S(1)} %get-tuple-element.64), channel_id=1, source_target_pairs={{0,4},{4,0},{8,12},{12,8},{16,20},{20,16},{24,28},{28,24},{1,5},{5... | collective-permute-start | bytes 1425416 | tf_op jit(solution)/shard_map/ppermute | solution.py:200
  284.3 16.1 %collective-permute-start.15 = (bf16[1856,128]{1,0:T(8,128)(2,1)S(1)}, bf16[1856,128]{1,0:T(8,128)(2,1)S(1)}, u32[]{:S(2)}, u32[]{:S(2)}) collective-permute-start(bf16[1856,128]{1,0:T(8,128)(2,1)S(1)} %get-tuple-element.62), channel_id=1, source_target_pairs={{0,4},{4,0},{8,12},{12,8},{16,20},{20,16},{24,28},{28,24},{1,5},{5... | collective-permute-start | bytes 1425416 | tf_op jit(solution)/shard_map/ppermute | solution.py:200
  294.8 19.2 %collective-permute-start.17 = (bf16[1856,128]{1,0:T(8,128)(2,1)}, bf16[1856,128]{1,0:T(8,128)(2,1)}, u32[]{:S(2)}, u32[]{:S(2)}) collective-permute-start(bf16[1856,128]{1,0:T(8,128)(2,1)} %get-tuple-element.114), channel_id=1, source_target_pairs={{0,8},{4,12},{8,16},{12,20},{16,24},{20,28},{1,9},{5,13},{9,17},{1... | collective-permute-start | bytes 1425416 | tf_op jit(solution)/shard_map/ppermute | solution.py:183
  297.5 16.5 %collective-permute-start.18 = (bf16[1856,128]{1,0:T(8,128)(2,1)}, bf16[1856,128]{1,0:T(8,128)(2,1)}, u32[]{:S(2)}, u32[]{:S(2)}) collective-permute-start(bf16[1856,128]{1,0:T(8,128)(2,1)} %get-tuple-element.113), channel_id=1, source_target_pairs={{8,0},{12,4},{16,8},{20,12},{24,16},{28,20},{9,1},{13,5},{17,9},{2... | collective-permute-start | bytes 1425416 | tf_op jit(solution)/shard_map/ppermute | solution.py:184
  313.9 226.4 %reduce-scatter.8.cloned.1.call-start = ((), (), s32[]{:S(2)}) async-start(), calls=%async_computation.6 | async-start | bytes 2621440 | tf_op jit(solution)/shard_map/reduce_scatter | solution.py:204
  315.8 15.1 %collective-permute-start.19 = (bf16[1856,128]{1,0:T(8,128)(2,1)S(1)}, bf16[1856,128]{1,0:T(8,128)(2,1)S(1)}, u32[]{:S(2)}, u32[]{:S(2)}) collective-permute-start(bf16[1856,128]{1,0:T(8,128)(2,1)S(1)} %get-tuple-element.112), channel_id=1, source_target_pairs={{0,8},{4,12},{8,16},{12,20},{16,24},{20,28},{1,9},{5,13},{9,17},{1... | collective-permute-start | bytes 1425416 | tf_op jit(solution)/shard_map/ppermute | solution.py:183
  320.7 14.5 %collective-permute-start.20 = (bf16[1856,128]{1,0:T(8,128)(2,1)S(1)}, bf16[1856,128]{1,0:T(8,128)(2,1)S(1)}, u32[]{:S(2)}, u32[]{:S(2)}) collective-permute-start(bf16[1856,128]{1,0:T(8,128)(2,1)S(1)} %get-tuple-element.111), channel_id=1, source_target_pairs={{8,0},{12,4},{16,8},{20,12},{24,16},{28,20},{9,1},{13,5},{17,9},{2... | collective-permute-start | bytes 1425416 | tf_op jit(solution)/shard_map/ppermute | solution.py:184
  323.5 47.5 %collective-permute-start.25 = (bf16[1856,128]{1,0:T(8,128)(2,1)S(1)}, bf16[1856,128]{1,0:T(8,128)(2,1)S(1)}, u32[]{:S(2)}, u32[]{:S(2)}) collective-permute-start(bf16[1856,128]{1,0:T(8,128)(2,1)S(1)} %get-tuple-element.74), channel_id=1, source_target_pairs={{0,4},{4,0},{8,12},{12,8},{16,20},{20,16},{24,28},{28,24},{1,5},{5... | collective-permute-start | bytes 1425416 | tf_op jit(solution)/shard_map/ppermute | solution.py:200
  340.5 32.7 %collective-permute-start.26 = (bf16[1856,128]{1,0:T(8,128)(2,1)S(1)}, bf16[1856,128]{1,0:T(8,128)(2,1)S(1)}, u32[]{:S(2)}, u32[]{:S(2)}) collective-permute-start(bf16[1856,128]{1,0:T(8,128)(2,1)S(1)} %get-tuple-element.72), channel_id=1, source_target_pairs={{0,4},{4,0},{8,12},{12,8},{16,20},{20,16},{24,28},{28,24},{1,5},{5... | collective-permute-start | bytes 1425416 | tf_op jit(solution)/shard_map/ppermute | solution.py:200
  356.8 17.2 %collective-permute-start.27 = (bf16[1856,128]{1,0:T(8,128)(2,1)S(1)}, bf16[1856,128]{1,0:T(8,128)(2,1)S(1)}, u32[]{:S(2)}, u32[]{:S(2)}) collective-permute-start(bf16[1856,128]{1,0:T(8,128)(2,1)S(1)} %get-tuple-element.70), channel_id=1, source_target_pairs={{0,4},{4,0},{8,12},{12,8},{16,20},{20,16},{24,28},{28,24},{1,5},{5... | collective-permute-start | bytes 1425416 | tf_op jit(solution)/shard_map/ppermute | solution.py:200
  368.3 24.1 %collective-permute-start.28 = (bf16[1856,128]{1,0:T(8,128)(2,1)S(1)}, bf16[1856,128]{1,0:T(8,128)(2,1)S(1)}, u32[]{:S(2)}, u32[]{:S(2)}) collective-permute-start(bf16[1856,128]{1,0:T(8,128)(2,1)S(1)} %get-tuple-element.68), channel_id=1, source_target_pairs={{0,4},{4,0},{8,12},{12,8},{16,20},{20,16},{24,28},{28,24},{1,5},{5... | collective-permute-start | bytes 1425416 | tf_op jit(solution)/shard_map/ppermute | solution.py:200
  371.1 14.9 %collective-permute-start.30 = (bf16[1856,128]{1,0:T(8,128)(2,1)S(1)}, bf16[1856,128]{1,0:T(8,128)(2,1)S(1)}, u32[]{:S(2)}, u32[]{:S(2)}) collective-permute-start(bf16[1856,128]{1,0:T(8,128)(2,1)S(1)} %get-tuple-element.105), channel_id=1, source_target_pairs={{8,0},{12,4},{16,8},{20,12},{24,16},{28,20},{9,1},{13,5},{17,9},{2... | collective-permute-start | bytes 1425416 | tf_op jit(solution)/shard_map/ppermute | solution.py:184
  387.4 17.8 %collective-permute-start.31 = (bf16[1856,128]{1,0:T(8,128)(2,1)}, bf16[1856,128]{1,0:T(8,128)(2,1)S(1)}, u32[]{:S(2)}, u32[]{:S(2)}) collective-permute-start(bf16[1856,128]{1,0:T(8,128)(2,1)} %get-tuple-element.104), channel_id=1, source_target_pairs={{0,8},{4,12},{8,16},{12,20},{16,24},{20,28},{1,9},{5,13},{9,17},{1... | collective-permute-start | bytes 1425416 | tf_op jit(solution)/shard_map/ppermute | solution.py:183
  389.6 15.6 %collective-permute-start.32 = (bf16[1856,128]{1,0:T(8,128)(2,1)}, bf16[1856,128]{1,0:T(8,128)(2,1)S(1)}, u32[]{:S(2)}, u32[]{:S(2)}) collective-permute-start(bf16[1856,128]{1,0:T(8,128)(2,1)} %get-tuple-element.103), channel_id=1, source_target_pairs={{8,0},{12,4},{16,8},{20,12},{24,16},{28,20},{9,1},{13,5},{17,9},{2... | collective-permute-start | bytes 1425416 | tf_op jit(solution)/shard_map/ppermute | solution.py:184
  392.4 55.3 %collective-permute-start.37 = (bf16[1856,128]{1,0:T(8,128)(2,1)}, bf16[1856,128]{1,0:T(8,128)(2,1)}, u32[]{:S(2)}, u32[]{:S(2)}) collective-permute-start(bf16[1856,128]{1,0:T(8,128)(2,1)} %get-tuple-element.82), channel_id=1, source_target_pairs={{0,4},{4,0},{8,12},{12,8},{16,20},{20,16},{24,28},{28,24},{1,5},{5... | collective-permute-start | bytes 1425416 | tf_op jit(solution)/shard_map/ppermute | solution.py:200
  405.2 136.2 %reduce-scatter.10.cloned.1.call-start = ((), (), s32[]{:S(2)}) async-start(), calls=%async_computation.7 | async-start | bytes 2621440 | tf_op jit(solution)/shard_map/reduce_scatter | solution.py:204
  407.3 15.3 %collective-permute-start.33 = (bf16[1856,128]{1,0:T(8,128)(2,1)S(1)}, bf16[1856,128]{1,0:T(8,128)(2,1)S(1)}, u32[]{:S(2)}, u32[]{:S(2)}) collective-permute-start(bf16[1856,128]{1,0:T(8,128)(2,1)S(1)} %get-tuple-element.102), channel_id=1, source_target_pairs={{0,8},{4,12},{8,16},{12,20},{16,24},{20,28},{1,9},{5,13},{9,17},{1... | collective-permute-start | bytes 1425416 | tf_op jit(solution)/shard_map/ppermute | solution.py:183
  411.9 14.9 %collective-permute-start.34 = (bf16[1856,128]{1,0:T(8,128)(2,1)S(1)}, bf16[1856,128]{1,0:T(8,128)(2,1)S(1)}, u32[]{:S(2)}, u32[]{:S(2)}) collective-permute-start(bf16[1856,128]{1,0:T(8,128)(2,1)S(1)} %get-tuple-element.101), channel_id=1, source_target_pairs={{8,0},{12,4},{16,8},{20,12},{24,16},{28,20},{9,1},{13,5},{17,9},{2... | collective-permute-start | bytes 1425416 | tf_op jit(solution)/shard_map/ppermute | solution.py:184
  415.9 34.9 %collective-permute-start.38 = (bf16[1856,128]{1,0:T(8,128)(2,1)S(1)}, bf16[1856,128]{1,0:T(8,128)(2,1)S(1)}, u32[]{:S(2)}, u32[]{:S(2)}) collective-permute-start(bf16[1856,128]{1,0:T(8,128)(2,1)S(1)} %get-tuple-element.80), channel_id=1, source_target_pairs={{0,4},{4,0},{8,12},{12,8},{16,20},{20,16},{24,28},{28,24},{1,5},{5... | collective-permute-start | bytes 1425416 | tf_op jit(solution)/shard_map/ppermute | solution.py:200
  432.2 19.4 %collective-permute-start.39 = (bf16[1856,128]{1,0:T(8,128)(2,1)S(1)}, bf16[1856,128]{1,0:T(8,128)(2,1)S(1)}, u32[]{:S(2)}, u32[]{:S(2)}) collective-permute-start(bf16[1856,128]{1,0:T(8,128)(2,1)S(1)} %get-tuple-element.78), channel_id=1, source_target_pairs={{0,4},{4,0},{8,12},{12,8},{16,20},{20,16},{24,28},{28,24},{1,5},{5... | collective-permute-start | bytes 1425416 | tf_op jit(solution)/shard_map/ppermute | solution.py:200
  444.9 23.4 %collective-permute-start.40 = (bf16[1856,128]{1,0:T(8,128)(2,1)S(1)}, bf16[1856,128]{1,0:T(8,128)(2,1)S(1)}, u32[]{:S(2)}, u32[]{:S(2)}) collective-permute-start(bf16[1856,128]{1,0:T(8,128)(2,1)S(1)} %get-tuple-element.76), channel_id=1, source_target_pairs={{0,4},{4,0},{8,12},{12,8},{16,20},{20,16},{24,28},{28,24},{1,5},{5... | collective-permute-start | bytes 1425416 | tf_op jit(solution)/shard_map/ppermute | solution.py:200
  447.7 14.9 %collective-permute-start.42 = (bf16[1856,128]{1,0:T(8,128)(2,1)S(1)}, bf16[1856,128]{1,0:T(8,128)(2,1)S(1)}, u32[]{:S(2)}, u32[]{:S(2)}) collective-permute-start(bf16[1856,128]{1,0:T(8,128)(2,1)S(1)} %get-tuple-element.97), channel_id=1, source_target_pairs={{8,0},{12,4},{16,8},{20,12},{24,16},{28,20},{9,1},{13,5},{17,9},{2... | collective-permute-start | bytes 1425416 | tf_op jit(solution)/shard_map/ppermute | solution.py:184
  464.1 19.7 %collective-permute-start.43 = (bf16[1856,128]{1,0:T(8,128)(2,1)}, bf16[1856,128]{1,0:T(8,128)(2,1)}, u32[]{:S(2)}, u32[]{:S(2)}) collective-permute-start(bf16[1856,128]{1,0:T(8,128)(2,1)} %get-tuple-element.96), channel_id=1, source_target_pairs={{0,8},{4,12},{8,16},{12,20},{16,24},{20,28},{1,9},{5,13},{9,17},{1... | collective-permute-start | bytes 1425416 | tf_op jit(solution)/shard_map/ppermute | solution.py:183
  467.0 16.7 %collective-permute-start.44 = (bf16[1856,128]{1,0:T(8,128)(2,1)}, bf16[1856,128]{1,0:T(8,128)(2,1)}, u32[]{:S(2)}, u32[]{:S(2)}) collective-permute-start(bf16[1856,128]{1,0:T(8,128)(2,1)} %get-tuple-element.95), channel_id=1, source_target_pairs={{8,0},{12,4},{16,8},{20,12},{24,16},{28,20},{9,1},{13,5},{17,9},{2... | collective-permute-start | bytes 1425416 | tf_op jit(solution)/shard_map/ppermute | solution.py:184
  481.0 95.2 %reduce-scatter.12.cloned.1.call-start = ((), (), s32[]{:S(2)}) async-start(), calls=%async_computation.8 | async-start | bytes 2621440 | tf_op jit(solution)/shard_map/reduce_scatter | solution.py:204
  483.7 37.8 %collective-permute-start.49 = (bf16[1856,128]{1,0:T(8,128)(2,1)S(1)}, bf16[1856,128]{1,0:T(8,128)(2,1)S(1)}, u32[]{:S(2)}, u32[]{:S(2)}) collective-permute-start(bf16[1856,128]{1,0:T(8,128)(2,1)S(1)} %get-tuple-element.90), channel_id=1, source_target_pairs={{0,4},{4,0},{8,12},{12,8},{16,20},{20,16},{24,28},{28,24},{1,5},{5... | collective-permute-start | bytes 1425416 | tf_op jit(solution)/shard_map/ppermute | solution.py:200
  488.7 14.9 %collective-permute-start.46 = (bf16[1856,128]{1,0:T(8,128)(2,1)S(1)}, bf16[1856,128]{1,0:T(8,128)(2,1)S(1)}, u32[]{:S(2)}, u32[]{:S(2)}) collective-permute-start(bf16[1856,128]{1,0:T(8,128)(2,1)S(1)} %get-tuple-element.93), channel_id=1, source_target_pairs={{8,0},{12,4},{16,8},{20,12},{24,16},{28,20},{9,1},{13,5},{17,9},{2... | collective-permute-start | bytes 1425416 | tf_op jit(solution)/shard_map/ppermute | solution.py:184
  492.4 30.0 %collective-permute-start.50 = (bf16[1856,128]{1,0:T(8,128)(2,1)S(1)}, bf16[1856,128]{1,0:T(8,128)(2,1)S(1)}, u32[]{:S(2)}, u32[]{:S(2)}) collective-permute-start(bf16[1856,128]{1,0:T(8,128)(2,1)S(1)} %get-tuple-element.88), channel_id=1, source_target_pairs={{0,4},{4,0},{8,12},{12,8},{16,20},{20,16},{24,28},{28,24},{1,5},{5... | collective-permute-start | bytes 1425416 | tf_op jit(solution)/shard_map/ppermute | solution.py:200
  (59 other events, 782.9 us)
Sparse Core Ops, SparseCore 0:
  314.0 40.0 reduce-scatter.5
  405.3 40.9 reduce-scatter.7
  481.1 40.7 reduce-scatter.9
  536.8 39.3 reduce-scatter.11

commit v2 on v1

--- a/solution.py
+++ b/solution.py
@@ -9,7 +9,7 @@
 
 TILE = 64
 LANES = 128
-CHUNKS = 4
+CHUNKS = 2
 SHARE = (3, 5)
 BLOCK = 256
 
@@ -84,8 +84,8 @@
         to = pl.multiple_of(row * TILE, TILE)
         for col in range(pairs):
             at = first + row * pairs + col
-            even = pl.multiple_of(rank_ref[0, at], TILE)
-            odd = pl.multiple_of(rank_ref[1, at], TILE)
+            even = pl.multiple_of(rank_ref[0, at], 16)
+            odd = pl.multiple_of(rank_ref[1, at], 16)
             dense_ref[pl.ds(to, TILE), col * LANES : (col + 1) * LANES] = (
                 packed_ref[pl.ds(even, TILE), :] * left + packed_ref[pl.ds(odd, TILE), :] * right
             )
@@ -133,7 +133,9 @@
     pairs = depth // LANES
     slots = -(-(rows // TILE) * pairs * SHARE[0] // (SHARE[1] * 2 * CHUNKS)) * 2 * CHUNKS
     half = slots // 2 * TILE
-    piece = half // CHUNKS
+    note = -(-amp_pattern.shape[0] // 16) * 16
+    piece = half // CHUNKS + note
+    share = piece * CHUNKS
 
     me = lax.axis_index("long")
     chip, core = me // 2, me % 2
@@ -147,17 +149,12 @@
     spots = jnp.stack([spot // pairs * TILE, spot % pairs * LANES], 1).reshape(4, slots)
     packed = pack(amplitudes, spots.astype(jnp.int32), slots)
 
-    patterns = lax.all_gather(amp_pattern, ("long", "grp"))
-    patterns = patterns.reshape(long, grp, *amp_pattern.shape)[owners]
-    full = jnp.any(jnp.sum(by_parity(patterns)[0], axis=-1) > slots)
-    here, count = by_parity(lax.dynamic_index_in_dim(patterns, lax.axis_index("grp"), 1, False))
-    rank = (count - 1 + core * (slots // 2)) % slots
-    ranks = jnp.where(here > 0, jnp.minimum(rank, slots), slots).astype(jnp.int32) * TILE
-
     sparse_int = integrals * spread(int_pattern, integrals.dtype)
 
-    keep = lax.dynamic_slice_in_dim(packed, core * half, half, 0)
-    give = lax.dynamic_slice_in_dim(packed, (1 - core) * half, half, 0)
+    tail = amp_pattern.astype(amplitudes.dtype)
+    tail = jnp.pad(tail, ((0, share - half - tail.shape[0]), (0, LANES - tail.shape[1])))
+    keep = jnp.concatenate([lax.dynamic_slice_in_dim(packed, core * half, half, 0), tail], 0)
+    give = jnp.concatenate([lax.dynamic_slice_in_dim(packed, (1 - core) * half, half, 0), tail], 0)
     gain = lax.ppermute(give, "long", swap)
 
     def own(number):
@@ -184,6 +181,7 @@
         fell.append(lax.ppermute(falling, "long", down))
 
     results = []
+    most = 0
     for step in range(steps):
         source = owners[step] // 2
         kept = []
@@ -197,16 +195,25 @@
                     above = (chip == place) & (source > chip)
                     value = jnp.where(above, fell[number + chips - 2 - place], value)
             kept.append(value)
+        start = half - (CHUNKS - 1) * piece
+        pattern = kept[-1][start : start + amp_pattern.shape[0], : amp_pattern.shape[1]]
+        here, count = by_parity(pattern.astype(jnp.int32))
+        most = jnp.maximum(most, jnp.max(jnp.sum(here, axis=-1)))
+        rank = jnp.maximum(count - 1, 0)
+        near = (rank // (slots // 2)) == core
+        at = rank % (slots // 2) * TILE + jnp.where(near, 0, share)
+        ranks = jnp.where((here > 0) & (rank < slots), at, 2 * share).astype(jnp.int32)
         other = [lax.ppermute(value, "long", swap) for value in kept]
         nothing = jnp.zeros((TILE, LANES), amplitudes.dtype)
         panel = jnp.concatenate(kept + other + [nothing], 0)
-        partial_value = multiply(panel, ranks[step], sparse_int, rows)
+        partial_value = multiply(panel, ranks, sparse_int, rows)
         total = lax.psum_scatter(partial_value, "grp", scatter_dimension=1, tiled=True)
         results.append(total.astype(amplitudes.dtype))
     quick = jnp.stack(results, 0)
 
+    over = lax.psum((most > slots).astype(jnp.float32), "grp")
     return lax.cond(
-        full,
+        over > 0,
         lambda: dense_path(amplitudes, sparse_int, amp_pattern, owners),
         lambda: quick,
     )

time: 597 us -> 563 us (0.943); the launches traced: 586 us -> 560 us
  waiting for transfers between devices: 164 us -> 230 us
  blocking collectives: 76 us -> 10.5 us
  between operations: 118 us -> 75.7 us
  other arithmetic: 60 us -> 92.5 us
  starting transfers between devices: 82.5 us -> 62.3 us
    all_gather x1 -> x0, blocking collectives: 76 us -> none  [per_device(): patterns = lax.all_gather(amp_pattern, ('long', 'grp'))]
    ppermute x18 -> x10, waiting for transfers between devices: 50.2 us -> 116 us  [per_device(): fell.append(lax.ppermute(falling, 'long', down))]
    select_n x19 -> x15, other arithmetic: 24.2 us -> 40.6 us  [outgoing(): jnp.where(mine, own(number), carried)]
    ppermute x18 -> x10, starting transfers between devices: 23.9 us -> 12.9 us  [per_device(): fell.append(lax.ppermute(falling, 'long', down))]
    psum x0 -> x1, blocking collectives: none -> 10.5 us  [per_device(): over = lax.psum((most > slots).astype(jnp.float32), 'grp')]
    ppermute x18 -> x10, waiting for transfers between devices: 79 us -> 88.7 us  [per_device(): rose.append(lax.ppermute(rising, 'long', up))]
    reduce_scatter x4, waiting for transfers between devices: 33.8 us -> 24.2 us  [per_device(): lax.psum_scatter(partial_value, 'grp', scatter_dimension=1, tiled=True)]
    ppermute x18 -> x10, starting transfers between devices: 57.4 us -> 48.5 us  [per_device(): rose.append(lax.ppermute(rising, 'long', up))]
  transfers between devices with their start and end apart: 57 -> 33, of which waited for: 28 -> 17; matrix products, arithmetic and copies ran while one was open for 13% -> 16% of each run, Pallas kernels for 8% -> 8%
where the time goes in v2:
time: 563 us; the launch traced here: 560 us
  waiting for transfers between devices  230 us (41%)
  other arithmetic  92.5 us (16%)
  between operations  75.7 us (13%)
  starting transfers between devices  62.3 us (11%)
  Pallas kernels  53.7 us (10%)
  local copies, waits for them, and re-layouts  29.9 us (5%)
  blocking collectives  10.5 us (2%)
    ppermute x10, waiting for transfers between devices, per_device(): fell.append(lax.ppermute(falling, 'long', down))  116 us
    ppermute x10, waiting for transfers between devices, per_device(): rose.append(lax.ppermute(rising, 'long', up))  88.7 us
    ppermute x10, starting transfers between devices, per_device(): rose.append(lax.ppermute(rising, 'long', up))  48.5 us
    pallas_call x4, Pallas kernels, multiply(): pl.pallas_call(functools.partial(multiply_kernel, depth // LANES), out_sh...  45.2 us
    select_n x15, other arithmetic, outgoing(): jnp.where(mine, own(number), carried)  40.6 us
    unnamed x17, other arithmetic  29.1 us
    reduce_scatter x4, waiting for transfers between devices, per_device(): lax.psum_scatter(partial_value, 'grp', scatter_dimension=1, tiled=True)  24.2 us
    unnamed x45, local copies, waits for them, and re-layouts  20.4 us
  transfers between devices with their start and end apart: 33, of which 17 were waited for; matrix products, arithmetic and copies ran while one was open for 16% of the time, Pallas kernels for 8%

profile of v2, /device:TPU:0, one launch (start us, length us, event | category | flops | bytes accessed | tf_op | source)
XLA Modules:
  0.0 559.7 jit_solution(16989363590733803839)
XLA Ops:
  10.1 8.4 %shard_map.57 = bf16[14848,128]{1,0:T(8,128)(2,1)} custom-call(s32[4,232]{1,0:T(4,128)} %reshape.347.where_ref, bf16[1024,3072]{1,0:T(8,128)(2,1)} %a_ref.1), custom_call_target="tpu_custom_call" | custom-call | tf_op jit(solution)/shard_map/pallas_call | solution.py:66
  34.1 22.0 %collective-permute-done.5 = bf16[3728,128]{1,0:T(8,128)(2,1)S(1)} collective-permute-done((bf16[3728,128]{1,0:T(8,128)(2,1)}, bf16[3728,128]{1,0:T(8,128)(2,1)S(1)}, u32[]{:S(2)}, u32[]{:S(2)}) %collective-permute-start.5) | collective-permute-done | bytes 954400 | tf_op jit(solution)/shard_map/ppermute | solution.py:181
  63.3 20.9 %collective-permute-done.6 = bf16[3728,128]{1,0:T(8,128)(2,1)S(1)} collective-permute-done((bf16[3728,128]{1,0:T(8,128)(2,1)}, bf16[3728,128]{1,0:T(8,128)(2,1)S(1)}, u32[]{:S(2)}, u32[]{:S(2)}) %collective-permute-start.6) | collective-permute-done | bytes 954400 | tf_op jit(solution)/shard_map/ppermute | solution.py:181
  91.4 20.1 %collective-permute-done.7 = bf16[3728,128]{1,0:T(8,128)(2,1)S(1)} collective-permute-done((bf16[3728,128]{1,0:T(8,128)(2,1)}, bf16[3728,128]{1,0:T(8,128)(2,1)S(1)}, u32[]{:S(2)}, u32[]{:S(2)}) %collective-permute-start.7) | collective-permute-done | bytes 954400 | tf_op jit(solution)/shard_map/ppermute | solution.py:181
  118.1 19.0 %collective-permute-done.8 = bf16[3728,128]{1,0:T(8,128)(2,1)} collective-permute-done((bf16[3728,128]{1,0:T(8,128)(2,1)}, bf16[3728,128]{1,0:T(8,128)(2,1)}, u32[]{:S(2)}, u32[]{:S(2)}) %collective-permute-start.8) | collective-permute-done | bytes 954400 | tf_op jit(solution)/shard_map/ppermute | solution.py:181
  143.5 18.4 %collective-permute-done.11 = bf16[3728,128]{1,0:T(8,128)(2,1)} collective-permute-done((bf16[3728,128]{1,0:T(8,128)(2,1)}, bf16[3728,128]{1,0:T(8,128)(2,1)}, u32[]{:S(2)}, u32[]{:S(2)}) %collective-permute-start.11) | collective-permute-done | bytes 954400 | tf_op jit(solution)/shard_map/ppermute | solution.py:181
  170.3 15.7 %collective-permute-done.12 = bf16[3728,128]{1,0:T(8,128)(2,1)} collective-permute-done((bf16[3728,128]{1,0:T(8,128)(2,1)}, bf16[3728,128]{1,0:T(8,128)(2,1)}, u32[]{:S(2)}, u32[]{:S(2)}) %collective-permute-start.12) | collective-permute-done | bytes 954400 | tf_op jit(solution)/shard_map/ppermute | solution.py:181
  195.2 12.5 %collective-permute-done.1 = bf16[3728,128]{1,0:T(8,128)(2,1)} collective-permute-done((bf16[3728,128]{1,0:T(8,128)(2,1)}, bf16[3728,128]{1,0:T(8,128)(2,1)}, u32[]{:S(2)}, u32[]{:S(2)}) %collective-permute-start.1) | collective-permute-done | bytes 954400 | tf_op jit(solution)/shard_map/ppermute | solution.py:180
  210.3 5.6 %collective-permute-start.2 = (bf16[3728,128]{1,0:T(8,128)(2,1)}, bf16[3728,128]{1,0:T(8,128)(2,1)}, u32[]{:S(2)}, u32[]{:S(2)}) collective-permute-start(bf16[3728,128]{1,0:T(8,128)(2,1)} %select_select_fusion.23), channel_id=1, source_target_pairs={{0,8},{4,12},{8,16},{12,20},{16,24},{20,28},{1,9},{5,13},{9,17},{1... | collective-permute-start | bytes 2863112 | tf_op jit(solution)/shard_map/ppermute | solution.py:180
  218.4 11.6 %collective-permute-done.2 = bf16[3728,128]{1,0:T(8,128)(2,1)} collective-permute-done((bf16[3728,128]{1,0:T(8,128)(2,1)}, bf16[3728,128]{1,0:T(8,128)(2,1)}, u32[]{:S(2)}, u32[]{:S(2)}) %collective-permute-start.2) | collective-permute-done | bytes 954400 | tf_op jit(solution)/shard_map/ppermute | solution.py:180
  232.8 5.3 collective-permute-start.3
  272.8 5.1 convolution_multiply_fusion.1.b_ref
  281.2 4.9 collective-permute-start.4
  289.7 9.5 %collective-permute-done.4 = bf16[3728,128]{1,0:T(8,128)(2,1)S(1)} collective-permute-done((bf16[3728,128]{1,0:T(8,128)(2,1)S(1)}, bf16[3728,128]{1,0:T(8,128)(2,1)S(1)}, u32[]{:S(2)}, u32[]{:S(2)}) %collective-permute-start.4) | collective-permute-done | bytes 954400 | tf_op jit(solution)/shard_map/ppermute | solution.py:180
  303.6 4.1 select_select_fusion.10
  307.8 6.6 %collective-permute-start.9 = (bf16[3728,128]{1,0:T(8,128)(2,1)}, bf16[3728,128]{1,0:T(8,128)(2,1)}, u32[]{:S(2)}, u32[]{:S(2)}) collective-permute-start(bf16[3728,128]{1,0:T(8,128)(2,1)} %get-tuple-element.80), channel_id=1, source_target_pairs={{0,8},{4,12},{8,16},{12,20},{16,24},{20,28},{1,9},{5,13},{9,17},{1... | collective-permute-start | bytes 2863112 | tf_op jit(solution)/shard_map/ppermute | solution.py:180
  321.4 11.3 %shard_map.58 = f32[1024,512]{1,0:T(8,128)} custom-call(s32[2,384]{1,0:T(2,128)} %fusion.30.rank_ref, bf16[14976,128]{1,0:T(8,128)(2,1)} %constant_dynamic-update-slice_fusion.packed_ref, bf16[3072,512]{1,0:T(8,128)(2,1)} %convolution_multiply_fusion.1.b_ref), custom_call_target="tpu_custom_call" | custom-call | flops 3221225472 | bytes 9076736 | tf_op jit(solution)/shard_map/pallas_call | solution.py:101
  336.7 4.3 collective-permute-start.10
  341.0 3.9 constant_dynamic-update-slice_fusion.9
  344.9 16.2 %collective-permute-done.10 = bf16[3728,128]{1,0:T(8,128)(2,1)S(1)} collective-permute-done((bf16[3728,128]{1,0:T(8,128)(2,1)S(1)}, bf16[3728,128]{1,0:T(8,128)(2,1)S(1)}, u32[]{:S(2)}, u32[]{:S(2)}) %collective-permute-start.10) | collective-permute-done | bytes 954400 | tf_op jit(solution)/shard_map/ppermute | solution.py:180
  361.1 3.8 constant_dynamic-update-slice_fusion.8
  377.8 17.0 %collective-permute-done.13 = bf16[3728,128]{1,0:T(8,128)(2,1)S(1)} collective-permute-done((bf16[3728,128]{1,0:T(8,128)(2,1)}, bf16[3728,128]{1,0:T(8,128)(2,1)S(1)}, u32[]{:S(2)}, u32[]{:S(2)}) %collective-permute-start.13) | collective-permute-done | bytes 954400 | tf_op jit(solution)/shard_map/ppermute | solution.py:180
  397.3 5.7 %collective-permute-start.14 = (bf16[3728,128]{1,0:T(8,128)(2,1)}, bf16[3728,128]{1,0:T(8,128)(2,1)}, u32[]{:S(2)}, u32[]{:S(2)}) collective-permute-start(bf16[3728,128]{1,0:T(8,128)(2,1)} %select_select_fusion.13), channel_id=1, source_target_pairs={{0,8},{4,12},{8,16},{12,20},{16,24},{20,28},{1,9},{5,13},{9,17},{1... | collective-permute-start | bytes 2863112 | tf_op jit(solution)/shard_map/ppermute | solution.py:180
  403.0 3.8 constant_dynamic-update-slice_fusion.14
  409.6 11.3 %shard_map.59 = f32[1024,512]{1,0:T(8,128)} custom-call(s32[2,384]{1,0:T(2,128)} %fusion.28.rank_ref, bf16[14976,128]{1,0:T(8,128)(2,1)} %constant_dynamic-update-slice_fusion.5.packed_ref, bf16[3072,512]{1,0:T(8,128)(2,1)} %convolution_multiply_fusion.1.b_ref), custom_call_target="tpu_custom_call" | custom-call | flops 3221225472 | bytes 9076736 | tf_op jit(solution)/shard_map/pallas_call | solution.py:101
  428.3 3.9 select_select_fusion.5
  440.0 16.7 %collective-permute-done.17 = bf16[3728,128]{1,0:T(8,128)(2,1)S(1)} collective-permute-done((bf16[3728,128]{1,0:T(8,128)(2,1)S(1)}, bf16[3728,128]{1,0:T(8,128)(2,1)S(1)}, u32[]{:S(2)}, u32[]{:S(2)}) %collective-permute-start.17) | collective-permute-done | bytes 954400 | tf_op jit(solution)/shard_map/ppermute | solution.py:180
  458.1 6.0 %collective-permute-start.18 = (bf16[3728,128]{1,0:T(8,128)(2,1)}, bf16[3728,128]{1,0:T(8,128)(2,1)}, u32[]{:S(2)}, u32[]{:S(2)}) collective-permute-start(bf16[3728,128]{1,0:T(8,128)(2,1)} %select_select_fusion.8), channel_id=1, source_target_pairs={{0,8},{4,12},{8,16},{12,20},{16,24},{20,28},{1,9},{5,13},{9,17},{1... | collective-permute-start | bytes 2863112 | tf_op jit(solution)/shard_map/ppermute | solution.py:180
  466.9 11.3 %shard_map.60 = f32[1024,512]{1,0:T(8,128)} custom-call(s32[2,384]{1,0:T(2,128)} %fusion.26.rank_ref, bf16[14976,128]{1,0:T(8,128)(2,1)} %constant_dynamic-update-slice_fusion.10.packed_ref, bf16[3072,512]{1,0:T(8,128)(2,1)} %convolution_multiply_fusion.1.b_ref), custom_call_target="tpu_custom_call" | custom-call | flops 3221225472 | bytes 9076736 | tf_op jit(solution)/shard_map/pallas_call | solution.py:101
  495.6 11.4 %shard_map.61 = f32[1024,512]{1,0:T(8,128)} custom-call(s32[2,384]{1,0:T(2,128)} %fusion.24.rank_ref, bf16[14976,128]{1,0:T(8,128)(2,1)} %constant_dynamic-update-slice_fusion.15.packed_ref, bf16[3072,512]{1,0:T(8,128)(2,1)} %convolution_multiply_fusion.1.b_ref), custom_call_target="tpu_custom_call" | custom-call | flops 3221225472 | bytes 9076736 | tf_op jit(solution)/shard_map/pallas_call | solution.py:101
  513.5 10.5 %psum.14 = f32[]{:T(128)} all-reduce(f32[]{:T(128)S(6)} %convert_element_type.45), channel_id=1, replica_groups=mesh['long'=8,'grp'=4] {'grp'}, use_global_device_ids=true, to_apply=%region_11.12 | all-reduce | flops 1 | bytes 8 | tf_op jit(solution)/shard_map/psum | solution.py:214
  526.9 24.1 %reduce-scatter.12.cloned.1.call-done = f32[1024,128]{1,0:T(8,128)} async-done(((f32[1024,512]{1,0:T(8,128)}), f32[1024,128]{1,0:T(8,128)}) %reduce-scatter.12.cloned.1.call-update) | async-done | bytes 524304 | tf_op jit(solution)/shard_map/reduce_scatter | solution.py:210
  (190 shorter events, 133.1 us)
Async XLA Ops:
  6.5 505.9 %reduce-scatter.6.cloned.1.call-start = ((), (), s32[]{:S(2)}) async-start(), calls=%async_computation.5 | async-start | bytes 2621440 | tf_op jit(solution)/shard_map/reduce_scatter | solution.py:210
  29.6 26.5 %collective-permute-start.5 = (bf16[3728,128]{1,0:T(8,128)(2,1)}, bf16[3728,128]{1,0:T(8,128)(2,1)S(1)}, u32[]{:S(2)}, u32[]{:S(2)}) collective-permute-start(bf16[3728,128]{1,0:T(8,128)(2,1)} %dynamic-slice_select_fusion), channel_id=1, source_target_pairs={{8,0},{12,4},{16,8},{20,12},{24,16},{28,20},{9,1},{13,5},{17,9},{2... | collective-permute-start | bytes 2863112 | tf_op jit(solution)/shard_map/ppermute | solution.py:181
  59.5 24.7 %collective-permute-start.6 = (bf16[3728,128]{1,0:T(8,128)(2,1)}, bf16[3728,128]{1,0:T(8,128)(2,1)S(1)}, u32[]{:S(2)}, u32[]{:S(2)}) collective-permute-start(bf16[3728,128]{1,0:T(8,128)(2,1)} %select_select_fusion.22), channel_id=1, source_target_pairs={{8,0},{12,4},{16,8},{20,12},{24,16},{28,20},{9,1},{13,5},{17,9},{2... | collective-permute-start | bytes 2863112 | tf_op jit(solution)/shard_map/ppermute | solution.py:181
  87.7 23.8 %collective-permute-start.7 = (bf16[3728,128]{1,0:T(8,128)(2,1)}, bf16[3728,128]{1,0:T(8,128)(2,1)S(1)}, u32[]{:S(2)}, u32[]{:S(2)}) collective-permute-start(bf16[3728,128]{1,0:T(8,128)(2,1)} %select_select_fusion.21), channel_id=1, source_target_pairs={{8,0},{12,4},{16,8},{20,12},{24,16},{28,20},{9,1},{13,5},{17,9},{2... | collective-permute-start | bytes 2863112 | tf_op jit(solution)/shard_map/ppermute | solution.py:181
  114.0 23.1 %collective-permute-start.8 = (bf16[3728,128]{1,0:T(8,128)(2,1)}, bf16[3728,128]{1,0:T(8,128)(2,1)}, u32[]{:S(2)}, u32[]{:S(2)}) collective-permute-start(bf16[3728,128]{1,0:T(8,128)(2,1)} %select_select_fusion.20), channel_id=1, source_target_pairs={{8,0},{12,4},{16,8},{20,12},{24,16},{28,20},{9,1},{13,5},{17,9},{2... | collective-permute-start | bytes 2863112 | tf_op jit(solution)/shard_map/ppermute | solution.py:181
  139.6 22.2 %collective-permute-start.11 = (bf16[3728,128]{1,0:T(8,128)(2,1)}, bf16[3728,128]{1,0:T(8,128)(2,1)}, u32[]{:S(2)}, u32[]{:S(2)}) collective-permute-start(bf16[3728,128]{1,0:T(8,128)(2,1)} %select_select_fusion.16), channel_id=1, source_target_pairs={{8,0},{12,4},{16,8},{20,12},{24,16},{28,20},{9,1},{13,5},{17,9},{2... | collective-permute-start | bytes 2863112 | tf_op jit(solution)/shard_map/ppermute | solution.py:181
  164.6 21.4 %collective-permute-start.12 = (bf16[3728,128]{1,0:T(8,128)(2,1)}, bf16[3728,128]{1,0:T(8,128)(2,1)}, u32[]{:S(2)}, u32[]{:S(2)}) collective-permute-start(bf16[3728,128]{1,0:T(8,128)(2,1)} %select_select_fusion.15), channel_id=1, source_target_pairs={{8,0},{12,4},{16,8},{20,12},{24,16},{28,20},{9,1},{13,5},{17,9},{2... | collective-permute-start | bytes 2863112 | tf_op jit(solution)/shard_map/ppermute | solution.py:181
  189.8 18.0 %collective-permute-start.1 = (bf16[3728,128]{1,0:T(8,128)(2,1)}, bf16[3728,128]{1,0:T(8,128)(2,1)}, u32[]{:S(2)}, u32[]{:S(2)}) collective-permute-start(bf16[3728,128]{1,0:T(8,128)(2,1)} %get-tuple-element.82), channel_id=1, source_target_pairs={{0,8},{4,12},{8,16},{12,20},{16,24},{20,28},{1,9},{5,13},{9,17},{1... | collective-permute-start | bytes 2863112 | tf_op jit(solution)/shard_map/ppermute | solution.py:180
  210.3 19.7 %collective-permute-start.2 = (bf16[3728,128]{1,0:T(8,128)(2,1)}, bf16[3728,128]{1,0:T(8,128)(2,1)}, u32[]{:S(2)}, u32[]{:S(2)}) collective-permute-start(bf16[3728,128]{1,0:T(8,128)(2,1)} %select_select_fusion.23), channel_id=1, source_target_pairs={{0,8},{4,12},{8,16},{12,20},{16,24},{20,28},{1,9},{5,13},{9,17},{1... | collective-permute-start | bytes 2863112 | tf_op jit(solution)/shard_map/ppermute | solution.py:180
  232.8 46.6 %collective-permute-start.3 = (bf16[3728,128]{1,0:T(8,128)(2,1)}, bf16[3728,128]{1,0:T(8,128)(2,1)}, u32[]{:S(2)}, u32[]{:S(2)}) collective-permute-start(bf16[3728,128]{1,0:T(8,128)(2,1)} %select_select_fusion.24), channel_id=1, source_target_pairs={{0,8},{4,12},{8,16},{12,20},{16,24},{20,28},{1,9},{5,13},{9,17},{1... | collective-permute-start | bytes 2863112 | tf_op jit(solution)/shard_map/ppermute | solution.py:180
  277.9 25.7 %collective-permute-start.15 = (bf16[3728,128]{1,0:T(8,128)(2,1)}, bf16[3728,128]{1,0:T(8,128)(2,1)}, u32[]{:S(2)}, u32[]{:S(2)}) collective-permute-start(bf16[3728,128]{1,0:T(8,128)(2,1)} %get-tuple-element.81), channel_id=1, source_target_pairs={{8,0},{12,4},{16,8},{20,12},{24,16},{28,20},{9,1},{13,5},{17,9},{2... | collective-permute-start | bytes 2863112 | tf_op jit(solution)/shard_map/ppermute | solution.py:181
  281.2 18.0 %collective-permute-start.4 = (bf16[3728,128]{1,0:T(8,128)(2,1)S(1)}, bf16[3728,128]{1,0:T(8,128)(2,1)S(1)}, u32[]{:S(2)}, u32[]{:S(2)}) collective-permute-start(bf16[3728,128]{1,0:T(8,128)(2,1)S(1)} %select_select_fusion.25), channel_id=1, source_target_pairs={{0,8},{4,12},{8,16},{12,20},{16,24},{20,28},{1,9},{5,13},{9,17},{1... | collective-permute-start | bytes 2863112 | tf_op jit(solution)/shard_map/ppermute | solution.py:180
  289.7 26.1 %collective-permute-start.21 = (bf16[3728,128]{1,0:T(8,128)(2,1)}, bf16[3728,128]{1,0:T(8,128)(2,1)}, u32[]{:S(2)}, u32[]{:S(2)}) collective-permute-start(bf16[3728,128]{1,0:T(8,128)(2,1)} %get-tuple-element.62), channel_id=1, source_target_pairs={{0,4},{4,0},{8,12},{12,8},{16,20},{20,16},{24,28},{28,24},{1,5},{5... | collective-permute-start | bytes 2863112 | tf_op jit(solution)/shard_map/ppermute | solution.py:206
  301.7 16.9 %collective-permute-start.22 = (bf16[3728,128]{1,0:T(8,128)(2,1)}, bf16[3728,128]{1,0:T(8,128)(2,1)}, u32[]{:S(2)}, u32[]{:S(2)}) collective-permute-start(bf16[3728,128]{1,0:T(8,128)(2,1)} %get-tuple-element.60), channel_id=1, source_target_pairs={{0,4},{4,0},{8,12},{12,8},{16,20},{20,16},{24,28},{28,24},{1,5},{5... | collective-permute-start | bytes 2863112 | tf_op jit(solution)/shard_map/ppermute | solution.py:206
  307.8 27.0 %collective-permute-start.9 = (bf16[3728,128]{1,0:T(8,128)(2,1)}, bf16[3728,128]{1,0:T(8,128)(2,1)}, u32[]{:S(2)}, u32[]{:S(2)}) collective-permute-start(bf16[3728,128]{1,0:T(8,128)(2,1)} %get-tuple-element.80), channel_id=1, source_target_pairs={{0,8},{4,12},{8,16},{12,20},{16,24},{20,28},{1,9},{5,13},{9,17},{1... | collective-permute-start | bytes 2863112 | tf_op jit(solution)/shard_map/ppermute | solution.py:180
  314.4 50.5 %collective-permute-start.16 = (bf16[3728,128]{1,0:T(8,128)(2,1)}, bf16[3728,128]{1,0:T(8,128)(2,1)}, u32[]{:S(2)}, u32[]{:S(2)}) collective-permute-start(bf16[3728,128]{1,0:T(8,128)(2,1)} %get-tuple-element.79), channel_id=1, source_target_pairs={{8,0},{12,4},{16,8},{20,12},{24,16},{28,20},{9,1},{13,5},{17,9},{2... | collective-permute-start | bytes 2863112 | tf_op jit(solution)/shard_map/ppermute | solution.py:181
  332.7 192.0 %reduce-scatter.8.cloned.1.call-start = ((), (), s32[]{:S(2)}) async-start(), calls=%async_computation.6 | async-start | bytes 2621440 | tf_op jit(solution)/shard_map/reduce_scatter | solution.py:210
  336.7 24.4 %collective-permute-start.10 = (bf16[3728,128]{1,0:T(8,128)(2,1)S(1)}, bf16[3728,128]{1,0:T(8,128)(2,1)S(1)}, u32[]{:S(2)}, u32[]{:S(2)}) collective-permute-start(bf16[3728,128]{1,0:T(8,128)(2,1)S(1)} %select_select_fusion.18), channel_id=1, source_target_pairs={{0,8},{4,12},{8,16},{12,20},{16,24},{20,28},{1,9},{5,13},{9,17},{1... | collective-permute-start | bytes 2863112 | tf_op jit(solution)/shard_map/ppermute | solution.py:180
  344.9 30.7 %collective-permute-start.23 = (bf16[3728,128]{1,0:T(8,128)(2,1)}, bf16[3728,128]{1,0:T(8,128)(2,1)}, u32[]{:S(2)}, u32[]{:S(2)}) collective-permute-start(bf16[3728,128]{1,0:T(8,128)(2,1)} %get-tuple-element.66), channel_id=1, source_target_pairs={{0,4},{4,0},{8,12},{12,8},{16,20},{20,16},{24,28},{28,24},{1,5},{5... | collective-permute-start | bytes 2863112 | tf_op jit(solution)/shard_map/ppermute | solution.py:206
  364.9 41.9 %collective-permute-start.24 = (bf16[3728,128]{1,0:T(8,128)(2,1)}, bf16[3728,128]{1,0:T(8,128)(2,1)}, u32[]{:S(2)}, u32[]{:S(2)}) collective-permute-start(bf16[3728,128]{1,0:T(8,128)(2,1)} %get-tuple-element.64), channel_id=1, source_target_pairs={{0,4},{4,0},{8,12},{12,8},{16,20},{20,16},{24,28},{28,24},{1,5},{5... | collective-permute-start | bytes 2863112 | tf_op jit(solution)/shard_map/ppermute | solution.py:206
  370.1 24.7 %collective-permute-start.13 = (bf16[3728,128]{1,0:T(8,128)(2,1)}, bf16[3728,128]{1,0:T(8,128)(2,1)S(1)}, u32[]{:S(2)}, u32[]{:S(2)}) collective-permute-start(bf16[3728,128]{1,0:T(8,128)(2,1)} %get-tuple-element.78), channel_id=1, source_target_pairs={{0,8},{4,12},{8,16},{12,20},{16,24},{20,28},{1,9},{5,13},{9,17},{1... | collective-permute-start | bytes 2863112 | tf_op jit(solution)/shard_map/ppermute | solution.py:180
  373.6 54.7 %collective-permute-start.19 = (bf16[3728,128]{1,0:T(8,128)(2,1)}, bf16[3728,128]{1,0:T(8,128)(2,1)}, u32[]{:S(2)}, u32[]{:S(2)}) collective-permute-start(bf16[3728,128]{1,0:T(8,128)(2,1)} %get-tuple-element.77), channel_id=1, source_target_pairs={{8,0},{12,4},{16,8},{20,12},{24,16},{28,20},{9,1},{13,5},{17,9},{2... | collective-permute-start | bytes 2863112 | tf_op jit(solution)/shard_map/ppermute | solution.py:181
  397.3 25.2 %collective-permute-start.14 = (bf16[3728,128]{1,0:T(8,128)(2,1)}, bf16[3728,128]{1,0:T(8,128)(2,1)}, u32[]{:S(2)}, u32[]{:S(2)}) collective-permute-start(bf16[3728,128]{1,0:T(8,128)(2,1)} %select_select_fusion.13), channel_id=1, source_target_pairs={{0,8},{4,12},{8,16},{12,20},{16,24},{20,28},{1,9},{5,13},{9,17},{1... | collective-permute-start | bytes 2863112 | tf_op jit(solution)/shard_map/ppermute | solution.py:180
  406.8 30.4 %collective-permute-start.25 = (bf16[3728,128]{1,0:T(8,128)(2,1)}, bf16[3728,128]{1,0:T(8,128)(2,1)}, u32[]{:S(2)}, u32[]{:S(2)}) collective-permute-start(bf16[3728,128]{1,0:T(8,128)(2,1)} %get-tuple-element.70), channel_id=1, source_target_pairs={{0,4},{4,0},{8,12},{12,8},{16,20},{20,16},{24,28},{28,24},{1,5},{5... | collective-permute-start | bytes 2863112 | tf_op jit(solution)/shard_map/ppermute | solution.py:206
  420.9 104.9 %reduce-scatter.10.cloned.1.call-start = ((), (), s32[]{:S(2)}) async-start(), calls=%async_computation.7 | async-start | bytes 2621440 | tf_op jit(solution)/shard_map/reduce_scatter | solution.py:210
  426.3 37.8 %collective-permute-start.26 = (bf16[3728,128]{1,0:T(8,128)(2,1)}, bf16[3728,128]{1,0:T(8,128)(2,1)}, u32[]{:S(2)}, u32[]{:S(2)}) collective-permute-start(bf16[3728,128]{1,0:T(8,128)(2,1)} %get-tuple-element.68), channel_id=1, source_target_pairs={{0,4},{4,0},{8,12},{12,8},{16,20},{20,16},{24,28},{28,24},{1,5},{5... | collective-permute-start | bytes 2863112 | tf_op jit(solution)/shard_map/ppermute | solution.py:206
  432.1 24.6 %collective-permute-start.17 = (bf16[3728,128]{1,0:T(8,128)(2,1)S(1)}, bf16[3728,128]{1,0:T(8,128)(2,1)S(1)}, u32[]{:S(2)}, u32[]{:S(2)}) collective-permute-start(bf16[3728,128]{1,0:T(8,128)(2,1)S(1)} %get-tuple-element.76), channel_id=1, source_target_pairs={{0,8},{4,12},{8,16},{12,20},{16,24},{20,28},{1,9},{5,13},{9,17},{1... | collective-permute-start | bytes 2863112 | tf_op jit(solution)/shard_map/ppermute | solution.py:180
  435.8 46.1 %collective-permute-start.20 = (bf16[3728,128]{1,0:T(8,128)(2,1)}, bf16[3728,128]{1,0:T(8,128)(2,1)}, u32[]{:S(2)}, u32[]{:S(2)}) collective-permute-start(bf16[3728,128]{1,0:T(8,128)(2,1)} %get-tuple-element.75), channel_id=1, source_target_pairs={{8,0},{12,4},{16,8},{20,12},{24,16},{28,20},{9,1},{13,5},{17,9},{2... | collective-permute-start | bytes 2863112 | tf_op jit(solution)/shard_map/ppermute | solution.py:181
  458.1 25.5 %collective-permute-start.18 = (bf16[3728,128]{1,0:T(8,128)(2,1)}, bf16[3728,128]{1,0:T(8,128)(2,1)}, u32[]{:S(2)}, u32[]{:S(2)}) collective-permute-start(bf16[3728,128]{1,0:T(8,128)(2,1)} %select_select_fusion.8), channel_id=1, source_target_pairs={{0,8},{4,12},{8,16},{12,20},{16,24},{20,28},{1,9},{5,13},{9,17},{1... | collective-permute-start | bytes 2863112 | tf_op jit(solution)/shard_map/ppermute | solution.py:180
  478.2 72.8 %reduce-scatter.12.cloned.1.call-start = ((), (), s32[]{:S(2)}) async-start(), calls=%async_computation.8 | async-start | bytes 2621440 | tf_op jit(solution)/shard_map/reduce_scatter | solution.py:210
  481.9 9.8 %collective-permute-start.27 = (bf16[3728,128]{1,0:T(8,128)(2,1)}, bf16[3728,128]{1,0:T(8,128)(2,1)}, u32[]{:S(2)}, u32[]{:S(2)}) collective-permute-start(bf16[3728,128]{1,0:T(8,128)(2,1)} %get-tuple-element.74), channel_id=1, source_target_pairs={{0,4},{4,0},{8,12},{12,8},{16,20},{20,16},{24,28},{28,24},{1,5},{5... | collective-permute-start | bytes 2863112 | tf_op jit(solution)/shard_map/ppermute | solution.py:206
  487.1 6.9 %collective-permute-start.28 = (bf16[3728,128]{1,0:T(8,128)(2,1)}, bf16[3728,128]{1,0:T(8,128)(2,1)S(1)}, u32[]{:S(2)}, u32[]{:S(2)}) collective-permute-start(bf16[3728,128]{1,0:T(8,128)(2,1)} %get-tuple-element.72), channel_id=1, source_target_pairs={{0,4},{4,0},{8,12},{12,8},{16,20},{20,16},{24,28},{28,24},{1,5},{5... | collective-permute-start | bytes 2863112 | tf_op jit(solution)/shard_map/ppermute | solution.py:206
  (19 other events, 280.2 us)
Sparse Core Ops, SparseCore 0:
  332.8 35.8 reduce-scatter.5
  421.0 34.1 reduce-scatter.7
  478.3 34.5 reduce-scatter.9
  515.7 35.1 reduce-scatter.11
